TPU v7x, 128 devices: a whole 4x4x4 slice. The times are simulated.
128 devices in a mesh: dp: 8 (over x, core), tp: 16 (over y, z).
Axes of the slice: x: 4, y: 4, z: 4, core: 2. Of those that a mesh axis runs over, the one named last changes fastest.
Arguments:
- queries: bfloat16 [1024, 128, 576], P(('dp', 'tp')), may hold values from -10 to 10
- new_latent: bfloat16 [1024, 576], P(('dp', 'tp')), may hold values from -6 to 6
- resident: bfloat16 [768, 256, 576], P(('dp', 'tp')), may hold values from -6 to 6
- leaving: bfloat16 [256, 2, 256, 576], P(('dp', 'tp')), may hold values from -6 to 6
- res_len: int32 [768], P(('dp', 'tp')), may hold values from 1 to 256, as said below
- leave_len: int32 [128, 2], replicated, may hold values from 1 to 256, as said below
- mig_dest: int32 [128, 2], replicated, may hold values from 0 to 15, as said below
- stream: bfloat16 [1024, 7168], P(('dp', 'tp')), may hold values from -6 to 6
- dense_gain: float32 [7168], replicated, may hold values from 0.1 to 1.9
- w_gate: bfloat16 [7168, 18432], P('dp', 'tp'), may hold values from -0.0625 to 0.0625
- w_up: bfloat16 [7168, 18432], P('dp', 'tp'), may hold values from -0.0625 to 0.0625
- w_down: bfloat16 [18432, 7168], P('tp', 'dp'), may hold values from -0.046875 to 0.046875
- moe_gain: float32 [7168], replicated, may hold values from 0.1 to 1.9
- expert_gate: bfloat16 [16, 7168, 2048], P('tp', None, 'dp'), may hold values from -0.0625 to 0.0625
- expert_up: bfloat16 [16, 7168, 2048], P('tp', None, 'dp'), may hold values from -0.0625 to 0.0625
- expert_down: bfloat16 [16, 2048, 7168], P('tp', 'dp'), may hold values from -0.125 to 0.125
- expert_ids: int32 [1024, 8], P(('dp', 'tp')), may hold values from 0 to 15, all different within a row; in each aligned block of 8 rows (0 to 7, 8 to 15, ...) at most 5 rows name the same one
- gate_scores: float32 [1024, 8], P(('dp', 'tp')), may hold values from 0.05 to 1
Outputs:
- context: bfloat16 [1024, 128, 512], P(('dp', 'tp'))
- arrived: bfloat16 [256, 2, 256, 576], P(('dp', 'tp'))
- stream_out: bfloat16 [1024, 7168], P(('dp', 'tp'))
Inputs may be any that keep to these rules, and one draw needn't show every extreme that they name: `mig_dest`: each device sends its 2 leaving requests to 2 different other devices of its dp index, and every device receives exactly 2 requests. `res_len`: some request holds all 256 positions. `leave_len`: some request holds all 256 positions. `expert_ids`: among the 8 rows of one device no expert is chosen by more than 5 rows, a bound that some block reaches; a row names 8 different experts.
All inputs are finite; a program needn't handle non-finite values.
Results may differ from a plain program's by a relative error of at most 0.023.
Values may be sent and summed in bfloat16 or wider, within the bound.
A program may use at most 128 MiB of HBM per device.

v0:
```python
import jax
import jax.numpy as jnp
from jax import lax
from jax.sharding import PartitionSpec as P

VDIM = 512
QKD = 192
EPS = 1e-06
ROUTE_SCALE = 2.5


def rms_scale(rows, gain):
    values = rows.astype(jnp.float32)
    mean_square = jnp.mean(values * values, axis=-1, keepdims=True)
    return (values * lax.rsqrt(mean_square + EPS) * gain).astype(jnp.bfloat16)


def attend(queries, keys, lengths, newest):
    scale = QKD ** (-0.5)
    scores = jnp.einsum("rhl,rcl->rhc", queries, keys, preferred_element_type=jnp.float32) * scale
    positions = jnp.arange(keys.shape[1])
    valid = positions[None, None, :] < lengths[:, None, None]
    masked = jnp.where(valid, scores, -1e30)
    own_score = (
        jnp.einsum("rhl,rl->rh", queries, newest, preferred_element_type=jnp.float32) * scale
    )
    top = jnp.maximum(jnp.max(masked, axis=-1), own_score)
    expo = jnp.where(valid, jnp.exp(masked - top[..., None]), 0.0)
    own_expo = jnp.exp(own_score - top)
    total = jnp.sum(expo, axis=-1) + own_expo
    weights = (expo / total[..., None]).astype(jnp.bfloat16)
    own_weight = (own_expo / total).astype(jnp.bfloat16)
    context = jnp.einsum(
        "rhc,rcv->rhv", weights, keys[:, :, :VDIM], preferred_element_type=jnp.float32
    )
    context = context + own_weight.astype(jnp.float32)[..., None] * newest[:, None, :VDIM].astype(
        jnp.float32
    )
    return context.astype(jnp.bfloat16)


def on_device(
    queries,
    new_latent,
    resident,
    leaving,
    res_len,
    leave_len,
    mig_dest,
    stream,
    dense_gain,
    w_gate,
    w_up,
    w_down,
    moe_gain,
    expert_gate,
    expert_up,
    expert_down,
    expert_ids,
    gate_scores,
):
    tp_count = lax.axis_size("tp")
    dp_count = lax.axis_size("dp")
    tp_rank = lax.axis_index("tp")
    dp_rank = lax.axis_index("dp")
    moving = leaving.shape[0]
    device = dp_rank * tp_count + tp_rank
    peers = jnp.arange(tp_count)
    own_dest = lax.dynamic_index_in_dim(mig_dest, device, 0, keepdims=False)
    outgoing = jnp.zeros((tp_count,) + leaving.shape[1:], jnp.bfloat16)
    for slot in range(moving):
        outgoing = jnp.where(
            (peers == own_dest[slot])[:, None, None, None], leaving[slot][None], outgoing
        )
    incoming = lax.all_to_all(outgoing, "tp", split_axis=0, concat_axis=0, tiled=True)
    group_dest = lax.dynamic_slice_in_dim(mig_dest, dp_rank * tp_count, tp_count, 0)
    group_len = lax.dynamic_slice_in_dim(leave_len, dp_rank * tp_count, tp_count, 0)
    match = group_dest == tp_rank
    is_source = jnp.any(match, axis=1)
    which = jnp.sum(jnp.where(match, jnp.arange(moving)[None, :], 0), axis=1)
    order = jnp.cumsum(is_source.astype(jnp.int32)) - 1
    arrivals = []
    arrival_len = []
    for arrival in range(moving):
        pick = is_source & (order == arrival)
        source = jnp.sum(jnp.where(pick, peers, 0))
        slot = jnp.sum(jnp.where(pick, which, 0))
        arrivals.append(lax.dynamic_index_in_dim(incoming, source, 0, keepdims=False))
        source_len = lax.dynamic_index_in_dim(group_len, source, 0, keepdims=False)
        arrival_len.append(lax.dynamic_index_in_dim(source_len, slot, 0, keepdims=False))
    arrived = jnp.stack(arrivals, axis=0)
    arrived_len = jnp.stack(arrival_len, axis=0)
    stay = resident.shape[0]
    context_stay = attend(queries[:stay], resident, res_len, new_latent[:stay])
    context_moved = attend(queries[stay:], arrived[:, 0], arrived_len, new_latent[stay:])
    context = jnp.concatenate([context_stay, context_moved], axis=0)
    rows_dev = stream.shape[0]
    width = stream.shape[1]
    normed = rms_scale(stream, dense_gain)
    nearby = lax.all_gather(normed[None], "tp", axis=0, tiled=True)
    gathered = lax.all_to_all(nearby[:, None], "dp", split_axis=3, concat_axis=1, tiled=True)
    features = gathered.reshape(-1, gathered.shape[-1])
    gate_part = jnp.dot(features, w_gate, preferred_element_type=jnp.float32)
    up_part = jnp.dot(features, w_up, preferred_element_type=jnp.float32)
    gate, up = (
        lax.psum(gate_part.astype(jnp.bfloat16), "dp").astype(jnp.float32),
        lax.psum(up_part.astype(jnp.bfloat16), "dp").astype(jnp.float32),
    )
    hidden_all = (jax.nn.silu(gate) * up).astype(jnp.bfloat16)
    block = hidden_all
    ffn_share = lax.psum_scatter(
        jnp.dot(block, w_down, preferred_element_type=jnp.float32).astype(jnp.bfloat16),
        "tp",
        scatter_dimension=0,
        tiled=True,
    ).astype(jnp.float32)
    ffn_rows = lax.all_to_all(
        ffn_share.reshape(dp_count, rows_dev, ffn_share.shape[-1]).astype(jnp.bfloat16),
        "dp",
        split_axis=0,
        concat_axis=2,
        tiled=True,
    ).astype(jnp.float32)
    middle = (stream.astype(jnp.float32) + ffn_rows[0]).astype(jnp.bfloat16)
    mixed = rms_scale(middle, moe_gain)
    experts = expert_gate.shape[0] * tp_count
    top_count = expert_ids.shape[1]
    capacity = min(rows_dev, rows_dev * top_count // experts + 1)
    hits = (expert_ids[:, :, None] == jnp.arange(experts)[None, None, :]).astype(jnp.int32)
    row_hits = jnp.sum(hits, axis=1)
    before = jnp.cumsum(row_hits, axis=0) - row_hits
    slot_of = jnp.sum(hits * before[:, None, :], axis=2)
    target = expert_ids * capacity + slot_of
    placed = jnp.any(target[:, :, None] == jnp.arange(experts * capacity)[None, None, :], axis=1)
    outgoing_rows = jnp.dot(
        placed.T.astype(jnp.bfloat16), mixed, preferred_element_type=jnp.float32
    )
    outgoing_rows = outgoing_rows.astype(jnp.bfloat16).reshape(experts, capacity, width)
    received = lax.all_to_all(outgoing_rows, "tp", split_axis=0, concat_axis=0, tiled=True)
    pooled = lax.all_gather(received, "dp", axis=0, tiled=True)
    flat = pooled.reshape(-1, width)
    block = flat
    gate = jnp.dot(block, expert_gate[0], preferred_element_type=jnp.float32)
    up = jnp.dot(block, expert_up[0], preferred_element_type=jnp.float32)
    inner = (jax.nn.silu(gate) * up).astype(jnp.bfloat16)
    summed = lax.psum_scatter(
        jnp.dot(inner, expert_down[0], preferred_element_type=jnp.float32).astype(jnp.bfloat16),
        "dp",
        scatter_dimension=0,
        tiled=True,
    )
    results = summed.reshape(received.shape)
    returned = lax.all_to_all(results, "tp", split_axis=0, concat_axis=0, tiled=True)
    flat_back = returned.reshape(experts * capacity, width)
    picked = jnp.take(flat_back, target.reshape(-1), axis=0).reshape(rows_dev, top_count, width)
    shares = gate_scores / jnp.sum(gate_scores, axis=1, keepdims=True) * ROUTE_SCALE
    routed = jnp.einsum("rk,rkd->rd", shares, picked.astype(jnp.float32))
    stream_out = (middle.astype(jnp.float32) + routed).astype(jnp.bfloat16)
    return (context, arrived, stream_out)


def solution(mesh):
    placed = (
        P(("dp", "tp"), None, None),
        P(("dp", "tp"), None),
        P(("dp", "tp"), None, None),
        P(("dp", "tp"), None, None, None),
        P(("dp", "tp")),
        P(),
        P(),
        P(("dp", "tp"), None),
        P(),
        P("dp", "tp"),
        P("dp", "tp"),
        P("tp", "dp"),
        P(),
        P("tp", None, "dp"),
        P("tp", None, "dp"),
        P("tp", "dp", None),
        P(("dp", "tp"), None),
        P(("dp", "tp"), None),
    )
    return jax.shard_map(
        on_device,
        mesh=mesh,
        in_specs=placed,
        out_specs=(
            P(("dp", "tp"), None, None),
            P(("dp", "tp"), None, None, None),
            P(("dp", "tp"), None),
        ),
        check_vma=False,
    )
```

profile of v0, /device:TPU:0, one launch (start us, length us, event | category | flops | bytes accessed | tf_op | source)
XLA Modules:
  0.0 688.6 jit_solution(10923640459823760998)
XLA Ops:
  8.4 1.6 fusion.51
  10.2 47.7 %all-gather.6.cloned.1.call-done = bf16[128,7168]{1,0:T(8,128)(2,1)} async-done(((bf16[8,7168]{1,0:T(8,128)(2,1)}), bf16[128,7168]{1,0:T(8,128)(2,1)}) %all-gather.6.cloned.1.call-update) | async-done | bytes 1835024 | tf_op jit(solution)/shard_map/all_gather | solution.py:100
  57.8 13.7 %copy.81 = bf16[16,1,8,7168]{0,2,1,3:T(8,128)(2,1)} copy(bf16[16,1,8,7168]{3,2,0,1:T(8,128)(2,1)} %bitcast.99) | data formatting | bytes 3670016 | tf_op jit(solution)/shard_map/broadcast_in_dim | solution.py:101
  71.6 17.3 %reshape.231 = bf16[8,2,57344]{2,1,0:T(2,128)(2,1)} reshape(bf16[7168,1,8,16]{3,2,1,0:T(8,128)(2,1)} %bitcast.94) | data formatting | bytes 3670016
  88.8 28.8 %all_to_all.39 = bf16[8,2,57344]{2,1,0:T(2,128)(2,1)} all-to-all(bf16[8,2,57344]{2,1,0:T(2,128)(2,1)} %reshape.231), channel_id=1, replica_groups=mesh['dp'=8,'tp'=16] {'dp'}, dimensions={0} | all-to-all | bytes 3670016 | tf_op jit(solution)/shard_map/all_to_all | solution.py:101
  117.6 12.5 %reshape.232 = bf16[7168,1,8,16]{3,2,1,0:T(8,128)(2,1)} reshape(bf16[8,2,57344]{2,1,0:T(2,128)(2,1)} %all_to_all.39) | data formatting | bytes 3670016
  130.1 13.8 %copy.95 = bf16[16,1,8,8,896]{4,3,2,0,1:T(8,128)(2,1)} copy(bf16[16,1,8,8,896]{0,2,4,3,1:T(8,128)(2,1)} %bitcast.95) | data formatting | bytes 3670016 | tf_op jit(solution)/shard_map/all_to_all | solution.py:101
  143.9 1.8 copy.83
  145.8 4.1 convolution_convert_fusion.2
  149.8 4.1 convolution_convert_fusion.3
  154.0 71.9 %all-reduce.3.cloned.1.call-done = (bf16[1024,1152]{1,0:T(8,128)(2,1)}, bf16[1024,1152]{1,0:T(8,128)(2,1)}) async-done(((bf16[1024,1152]{1,0:T(8,128)(2,1)}, bf16[1024,1152]{1,0:T(8,128)(2,1)}), (bf16[1024,1152]{1,0:T(8,128)(2,1)}, bf16[1024,1152]{1,0:T(8,128)(2,1)})) %all-reduce.3.cloned.1.call-update) | async-done | bytes 4718608 | tf_op jit(solution)/shard_map/psum | solution.py:107
  225.9 7.3 %fusion.12 = bf16[1024,896]{1,0:T(8,128)(2,1)} fusion(bf16[1152,896]{1,0:T(8,128)(2,1)} %param.29, bf16[1024,1152]{1,0:T(8,128)(2,1)} %get-tuple-element.30, bf16[1024,1152]{1,0:T(8,128)(2,1)} %get-tuple-element.31), kind=kOutput, calls=%fused_computation.19 | convolution fusion | flops 2124283904 | bytes 8617984 | tf_op jit(solution)/shard_map/dot_general | solution.py:112
  233.7 75.1 %reduce-scatter.3.cloned.1.call-done = bf16[64,896]{1,0:T(8,128)(2,1)} async-done(((bf16[1024,896]{1,0:T(8,128)(2,1)}), bf16[64,896]{1,0:T(8,128)(2,1)}) %reduce-scatter.3.cloned.1.call-update) | async-done | bytes 114704 | tf_op jit(solution)/shard_map/reduce_scatter | solution.py:111
  308.7 4.3 all-to-all-start.2
  313.3 5.6 all-to-all-done.2
  320.2 29.9 %all_to_all.40 = bf16[16,5,7168]{2,1,0:T(8,128)(2,1)S(1)} all-to-all(bf16[16,5,7168]{2,1,0:T(8,128)(2,1)S(1)} %reshape.205), channel_id=1, replica_groups=mesh['dp'=8,'tp'=16] {'tp'}, dimensions={0} | all-to-all | bytes 2293760 | tf_op jit(solution)/shard_map/all_to_all | solution.py:139
  350.2 1.8 copy.84
  352.0 49.3 %all-gather.4.cloned.1.call-done = bf16[128,5,7168]{2,0,1:T(8,128)(2,1)} async-done(((bf16[16,5,7168]{2,0,1:T(8,128)(2,1)}), bf16[128,5,7168]{2,0,1:T(8,128)(2,1)}) %all-gather.4.cloned.1.call-update) | async-done | bytes 9175056 | tf_op jit(solution)/shard_map/all_gather | solution.py:140
  401.3 14.0 %copy.85 = bf16[128,5,7168]{2,1,0:T(8,128)(2,1)} copy(bf16[128,5,7168]{2,0,1:T(8,128)(2,1)} %all-gather.4.cloned.1.call-done) | data formatting | bytes 18350080 | tf_op jit(solution)/shard_map/all_gather | solution.py:140
  415.3 15.1 %reshape.206 = bf16[640,7168]{1,0:T(8,128)(2,1)} reshape(bf16[128,5,7168]{2,1,0:T(8,128)(2,1)} %copy.85) | data formatting | bytes 18350080 | tf_op jit(solution)/shard_map/reshape | solution.py:141
  430.4 7.2 %fusion.8 = f32[640,256]{1,0:T(8,128)S(1)} fusion(bf16[640,7168]{1,0:T(8,128)(2,1)} %reshape.206, bf16[1,7168,256]{2,1,0:T(8,128)(2,1)} %param.31), kind=kOutput, calls=%fused_computation.16 | convolution fusion | flops 2348810240 | bytes 13500416 | tf_op jit(solution)/shard_map/dot_general | solution.py:143
  437.6 18.9 %convolution_convert_fusion = bf16[640,7168]{1,0:T(8,128)(2,1)} fusion(bf16[1,256,7168]{2,1,0:T(8,128)(2,1)} %param.33, bf16[640,7168]{1,0:T(8,128)(2,1)} %reshape.206, bf16[1,7168,256]{2,1,0:T(8,128)(2,1)} %param.32, f32[640,256]{1,0:T(8,128)S(1)} %fusion.8), kind=kOutput, calls=%fused_computation.1 | convolution fusion | flops 4703191040 | bytes 26345472 | tf_op jit(solution)/shard_map/dot_general | solution.py:147
  459.1 4.9 select_select_fusion
  464.1 7.2 %all-to-all-start = ((bf16[16,2,256,576]{2,3,1,0:T(8,128)(2,1)}), bf16[16,2,256,576]{2,3,1,0:T(8,128)(2,1)}, u32[]{:S(2)}, u32[]{:S(2)}) async-start(bf16[16,2,256,576]{2,3,1,0:T(8,128)(2,1)} %select_select_fusion), calls=%async_computation | async-start | bytes 18874368 | tf_op jit(solution)/shard_map/all_to_all | solution.py:75
  482.3 2.2 fusion.88
  485.3 1.6 add_convert_fusion
  486.9 148.7 %all-to-all-done = bf16[16,2,256,576]{2,3,1,0:T(8,128)(2,1)} async-done(((bf16[16,2,256,576]{2,3,1,0:T(8,128)(2,1)}), bf16[16,2,256,576]{2,3,1,0:T(8,128)(2,1)}, u32[]{:S(2)}, u32[]{:S(2)}) %all-to-all-start) | async-done | bytes 9437216 | tf_op jit(solution)/shard_map/all_to_all | solution.py:75
  638.1 2.6 reshape.207
  640.7 10.5 %all-to-all-start.4 = ((bf16[16,5,7168]{2,1,0:T(8,128)(2,1)}), bf16[16,5,7168]{2,1,0:T(8,128)(2,1)S(1)}, u32[]{:S(2)}, u32[]{:S(2)}) async-start(bf16[16,5,7168]{2,1,0:T(8,128)(2,1)} %reshape.207), calls=%async_computation.6 | async-start | bytes 3670016 | tf_op jit(solution)/shard_map/all_to_all | solution.py:153
  654.1 23.0 %all-to-all-done.4 = bf16[16,5,7168]{2,1,0:T(8,128)(2,1)S(1)} async-done(((bf16[16,5,7168]{2,1,0:T(8,128)(2,1)}), bf16[16,5,7168]{2,1,0:T(8,128)(2,1)S(1)}, u32[]{:S(2)}, u32[]{:S(2)}) %all-to-all-start.4) | async-done | bytes 1146912 | tf_op jit(solution)/shard_map/all_to_all | solution.py:153
  677.7 2.1 gather_fusion
  679.7 1.6 fusion.31
  (101 shorter events, 17.0 us)
Async XLA Ops:
  7.2 138.6 %copy-start = (bf16[896,1152]{1,0:T(8,128)(2,1)S(1)}, bf16[896,1152]{1,0:T(8,128)(2,1)}, u32[]{:S(2)}) copy-start(bf16[896,1152]{1,0:T(8,128)(2,1)} %param.28) | copy-start | bytes 6193156
  7.2 50.6 %all-gather.6.cloned.1.call-start = ((), (), s32[]{:S(2)}) async-start(), calls=%async_computation.10 | async-start | bytes 1949696 | tf_op jit(solution)/shard_map/all_gather | solution.py:100
  10.1 215.8 %all-reduce.3.cloned.1.call-start = ((), (), s32[]{:S(2)}) async-start(), calls=%async_computation.11 | async-start | bytes 9437184 | tf_op jit(solution)/shard_map/psum | solution.py:107
  145.7 4.1 copy-start.16
  154.0 154.8 %reduce-scatter.3.cloned.1.call-start = ((), (), s32[]{:S(2)}) async-start(), calls=%async_computation.7 | async-start | bytes 1949696 | tf_op jit(solution)/shard_map/reduce_scatter | solution.py:111
  225.9 7.4 %copy-start.10 = (s32[8,8]{1,0:T(8,128)S(1)}, s32[8,8]{1,0:T(8,128)}, u32[]{:S(2)}) copy-start(s32[8,8]{1,0:T(8,128)} %param.34) | copy-start | bytes 772
  233.2 85.7 %copy-start.4 = (bf16[8,7168]{1,0:T(8,128)(2,1)S(1)}, bf16[8,7168]{1,0:T(8,128)(2,1)}, u32[]{:S(2)}) copy-start(bf16[8,7168]{1,0:T(8,128)(2,1)} %param.25) | copy-start | bytes 344068
  233.2 85.9 %copy-start.11 = (f32[7168]{0:T(1024)S(1)}, f32[7168]{0:T(1024)}, u32[]{:S(2)}) copy-start(f32[7168]{0:T(1024)} %param.30) | copy-start | bytes 86020
  308.7 10.2 %all-to-all-start.2 = ((bf16[8,8,896]{2,1,0:T(8,128)(2,1)}), bf16[8,8,896]{2,1,0:T(8,128)(2,1)S(1)}, u32[]{:S(2)}, u32[]{:S(2)}) async-start(bf16[8,8,896]{2,1,0:T(8,128)(2,1)} %bitcast.101), calls=%async_computation.3 | async-start | bytes 229376 | tf_op jit(solution)/shard_map/all_to_all | solution.py:117
  313.0 88.3 %all-gather.4.cloned.1.call-start = ((), (), s32[]{:S(2)}) async-start(), calls=%async_computation.8 | async-start | bytes 10321920 | tf_op jit(solution)/shard_map/all_gather | solution.py:140
  351.9 286.2 %reduce-scatter.5.cloned.1.call-start = ((), (), s32[]{:S(2)}) async-start(), calls=%async_computation.9 | async-start | bytes 10321920 | tf_op jit(solution)/shard_map/reduce_scatter | solution.py:146
  456.5 0.7 copy-start.13
  456.5 2.6 copy-start.3
  464.0 15.9 %copy-start.12 = (f32[8,8]{1,0:T(8,128)S(1)}, f32[8,8]{1,0:T(8,128)}, u32[]{:S(2)}) copy-start(f32[8,8]{1,0:T(8,128)} %param.35) | copy-start | bytes 772
  464.0 16.0 %copy-start.14 = (s32[128,2]{0,1:T(2,128)S(1)}, s32[128,2]{0,1:T(2,128)}, u32[]{:S(2)}) copy-start(s32[128,2]{0,1:T(2,128)} %param.23) | copy-start | bytes 3076
  464.0 18.0 %copy-start.15 = (s32[6]{0:T(128)S(1)}, s32[6]{0:T(128)}, u32[]{:S(2)}) copy-start(s32[6]{0:T(128)} %param.22) | copy-start | bytes 76
  464.0 18.1 %copy-start.9 = (bf16[8,576]{1,0:T(8,128)(2,1)S(1)}, bf16[8,576]{1,0:T(8,128)(2,1)}, u32[]{:S(2)}) copy-start(bf16[8,576]{1,0:T(8,128)(2,1)} %param.19) | copy-start | bytes 27652
  464.1 18.1 %copy-start.2 = (bf16[8,128,576]{1,2,0:T(8,128)(2,1)S(1)}, bf16[8,128,576]{1,2,0:T(8,128)(2,1)}, u32[]{:S(2)}) copy-start(bf16[8,128,576]{1,2,0:T(8,128)(2,1)} %param.18) | copy-start | bytes 3538948
  464.1 171.5 %all-to-all-start = ((bf16[16,2,256,576]{2,3,1,0:T(8,128)(2,1)}), bf16[16,2,256,576]{2,3,1,0:T(8,128)(2,1)}, u32[]{:S(2)}, u32[]{:S(2)}) async-start(bf16[16,2,256,576]{2,3,1,0:T(8,128)(2,1)} %select_select_fusion), calls=%async_computation | async-start | bytes 18874368 | tf_op jit(solution)/shard_map/all_to_all | solution.py:75
  482.3 2.9 copy-start.17
  637.0 3.7 copy-start.6
  640.7 36.4 %all-to-all-start.4 = ((bf16[16,5,7168]{2,1,0:T(8,128)(2,1)}), bf16[16,5,7168]{2,1,0:T(8,128)(2,1)S(1)}, u32[]{:S(2)}, u32[]{:S(2)}) async-start(bf16[16,5,7168]{2,1,0:T(8,128)(2,1)} %reshape.207), calls=%async_computation.6 | async-start | bytes 3670016 | tf_op jit(solution)/shard_map/all_to_all | solution.py:153
  651.2 1.2 copy-start.8
  651.2 1.4 copy-start.7
  651.3 1.8 copy-start.5
  677.7 4.4 copy-start.1
Sparse Core Ops, SparseCore 0:
  10.7 47.0 all-gather.5
  154.1 71.7 all-reduce.2
  233.4 75.3 reduce-scatter.2
  352.1 49.2 all-gather.3
  456.6 56.3 reduce-scatter.4
where the time goes:
time: 690 us; the launch traced here: 689 us
  waiting for transfers between devices  421 us (61%)
  local copies, waits for them, and re-layouts  100 us (14%)
  blocking collectives  58.7 us (9%)
  matrix products  49.5 us (7%)
  starting transfers between devices  22.3 us (3%)
  between operations  21.7 us (3%)
  other arithmetic  14.9 us (2%)
    all_to_all x1, waiting for transfers between devices, on_device(): lax.all_to_all(outgoing, 'tp', split_axis=0, concat_axis=0, tiled=True)  149 us
    reduce_scatter x1, waiting for transfers between devices, on_device(): lax.psum_scatter(jnp.dot(block, w_down, preferred_element_type=jnp.float3...  75.1 us
    psum x1, waiting for transfers between devices, on_device(): lax.psum(up_part.astype(jnp.bfloat16), 'dp').astype(jnp.float32)  71.9 us
    all_gather x1, waiting for transfers between devices, on_device(): pooled = lax.all_gather(received, 'dp', axis=0, tiled=True)  49.3 us
    all_gather x1, waiting for transfers between devices, on_device(): nearby = lax.all_gather(normed[None], 'tp', axis=0, tiled=True)  47.7 us
    unnamed x40, local copies, waits for them, and re-layouts  32.9 us
    all_to_all x1, blocking collectives, on_device(): lax.all_to_all(outgoing_rows, 'tp', split_axis=0, concat_axis=0, tiled=True)  29.9 us
    all_to_all x1, blocking collectives, on_device(): lax.all_to_all(nearby[:, None], 'dp', split_axis=3, concat_axis=1, tiled=...  28.8 us
  transfers between devices with their start and end apart: 8, of which 7 were waited for; matrix products, arithmetic and copies ran while one was open for 3% of the time, Pallas kernels for 0%

commit v1 on v0

--- a/solution.py
+++ b/solution.py
@@ -97,7 +97,9 @@
     rows_dev = stream.shape[0]
     width = stream.shape[1]
     normed = rms_scale(stream, dense_gain)
-    nearby = lax.all_gather(normed[None], "tp", axis=0, tiled=True)
+    nearby = jnp.concatenate(
+        lax.all_to_all(jnp.stack([normed[None]] * lax.axis_size("tp")), "tp", 0, 0), axis=0
+    )
     gathered = lax.all_to_all(nearby[:, None], "dp", split_axis=3, concat_axis=1, tiled=True)
     features = gathered.reshape(-1, gathered.shape[-1])
     gate_part = jnp.dot(features, w_gate, preferred_element_type=jnp.float32)

time: 690 us -> 675 us (0.978)
  waiting for transfers between devices: 421 us -> 373 us
  blocking collectives: 58.7 us -> 92.2 us
    all_gather x1 -> x0, waiting for transfers between devices: 47.7 us -> none  [on_device(): nearby = lax.all_gather(normed[None], 'tp', axis=0, tiled=True)]
    all_to_all x0 -> x1, blocking collectives: none -> 33.4 us  [on_device(): lax.all_to_all(jnp.stack([normed[None]] * lax.axis_size('tp')), 'tp', 0, 0)]
    all_to_all x0 -> x1, local copies, waits for them, and re-layouts: none -> 13.7 us  [on_device(): lax.all_to_all(jnp.stack([normed[None]] * lax.axis_size('tp')), 'tp', 0, 0)]
    broadcast_in_dim x1 -> x0, local copies, waits for them, and re-layouts: 13.7 us -> none  [on_device(): nearby[:, None]]
  transfers between devices with their start and end apart: 8 -> 7, of which waited for: 7 -> 6; matrix products, arithmetic and copies ran while one was open for 3% -> 3% of each run, Pallas kernels for 0% -> 0%
where the time goes in v1:
time: 675 us; the launch traced here: 673 us
  waiting for transfers between devices  373 us (55%)
  local copies, waits for them, and re-layouts  100 us (15%)
  blocking collectives  92.2 us (14%)
  matrix products  49.5 us (7%)
  starting transfers between devices  22.1 us (3%)
  between operations  21.7 us (3%)
  other arithmetic  14.2 us (2%)
    all_to_all x1, waiting for transfers between devices, on_device(): lax.all_to_all(outgoing, 'tp', split_axis=0, concat_axis=0, tiled=True)  149 us
    reduce_scatter x1, waiting for transfers between devices, on_device(): lax.psum_scatter(jnp.dot(block, w_down, preferred_element_type=jnp.float3...  75.1 us
    psum x1, waiting for transfers between devices, on_device(): lax.psum(up_part.astype(jnp.bfloat16), 'dp').astype(jnp.float32)  70.8 us
    all_gather x1, waiting for transfers between devices, on_device(): pooled = lax.all_gather(received, 'dp', axis=0, tiled=True)  49.3 us
    all_to_all x1, blocking collectives, on_device(): lax.all_to_all(jnp.stack([normed[None]] * lax.axis_size('tp')), 'tp', 0, 0)  33.4 us
    unnamed x40, local copies, waits for them, and re-layouts  32.9 us
    all_to_all x1, blocking collectives, on_device(): lax.all_to_all(outgoing_rows, 'tp', split_axis=0, concat_axis=0, tiled=True)  29.9 us
    all_to_all x1, blocking collectives, on_device(): lax.all_to_all(nearby[:, None], 'dp', split_axis=3, concat_axis=1, tiled=...  28.8 us
  transfers between devices with their start and end apart: 7, of which 6 were waited for; matrix products, arithmetic and copies ran while one was open for 3% of the time, Pallas kernels for 0%

profile of v1, /device:TPU:0, one launch (start us, length us, event | category | flops | bytes accessed | tf_op | source)
XLA Modules:
  0.0 672.8 jit_solution(1972821689849838458)
XLA Ops:
  9.6 33.4 %all_to_all.44 = bf16[16,1,8,7168]{3,2,1,0:T(8,128)(2,1)} all-to-all(bf16[16,1,8,7168]{3,2,1,0:T(8,128)(2,1)S(1)} %stack.15), channel_id=1, replica_groups=mesh['dp'=8,'tp'=16] {'tp'}, dimensions={0} | all-to-all | bytes 3670016 | tf_op jit(solution)/shard_map/all_to_all | solution.py:101
  43.1 13.7 %copy.71 = bf16[16,1,8,7168]{0,2,1,3:T(8,128)(2,1)} copy(bf16[16,1,8,7168]{3,2,1,0:T(8,128)(2,1)} %all_to_all.44) | data formatting | bytes 3670016 | tf_op jit(solution)/shard_map/all_to_all | solution.py:101
  56.8 17.3 %reshape.231 = bf16[8,2,57344]{2,1,0:T(2,128)(2,1)} reshape(bf16[7168,1,8,16]{3,2,1,0:T(8,128)(2,1)} %bitcast.93) | data formatting | bytes 3670016
  74.1 28.8 %all_to_all.45 = bf16[8,2,57344]{2,1,0:T(2,128)(2,1)} all-to-all(bf16[8,2,57344]{2,1,0:T(2,128)(2,1)} %reshape.231), channel_id=1, replica_groups=mesh['dp'=8,'tp'=16] {'dp'}, dimensions={0} | all-to-all | bytes 3670016 | tf_op jit(solution)/shard_map/all_to_all | solution.py:103
  102.9 12.5 %reshape.232 = bf16[7168,1,8,16]{3,2,1,0:T(8,128)(2,1)} reshape(bf16[8,2,57344]{2,1,0:T(2,128)(2,1)} %all_to_all.45) | data formatting | bytes 3670016
  115.4 13.8 %copy.85 = bf16[16,1,8,8,896]{4,3,2,0,1:T(8,128)(2,1)} copy(bf16[16,1,8,8,896]{0,2,4,3,1:T(8,128)(2,1)} %bitcast.94) | data formatting | bytes 3670016 | tf_op jit(solution)/shard_map/all_to_all | solution.py:103
  129.2 1.8 copy.73
  131.0 4.1 convolution_convert_fusion.2
  135.1 4.1 convolution_convert_fusion.3
  139.3 70.8 %all-reduce.3.cloned.1.call-done = (bf16[1024,1152]{1,0:T(8,128)(2,1)}, bf16[1024,1152]{1,0:T(8,128)(2,1)}) async-done(((bf16[1024,1152]{1,0:T(8,128)(2,1)}, bf16[1024,1152]{1,0:T(8,128)(2,1)}), (bf16[1024,1152]{1,0:T(8,128)(2,1)}, bf16[1024,1152]{1,0:T(8,128)(2,1)})) %all-reduce.3.cloned.1.call-update) | async-done | bytes 4718608 | tf_op jit(solution)/shard_map/psum | solution.py:109
  210.1 7.3 %fusion.12 = bf16[1024,896]{1,0:T(8,128)(2,1)} fusion(bf16[1152,896]{1,0:T(8,128)(2,1)} %param.29, bf16[1024,1152]{1,0:T(8,128)(2,1)} %get-tuple-element.27, bf16[1024,1152]{1,0:T(8,128)(2,1)} %get-tuple-element.28), kind=kOutput, calls=%fused_computation.19 | convolution fusion | flops 2124283904 | bytes 8617984 | tf_op jit(solution)/shard_map/dot_general | solution.py:114
  217.9 75.1 %reduce-scatter.3.cloned.1.call-done = bf16[64,896]{1,0:T(8,128)(2,1)} async-done(((bf16[1024,896]{1,0:T(8,128)(2,1)}), bf16[64,896]{1,0:T(8,128)(2,1)}) %reduce-scatter.3.cloned.1.call-update) | async-done | bytes 114704 | tf_op jit(solution)/shard_map/reduce_scatter | solution.py:113
  292.9 4.3 all-to-all-start.3
  297.3 5.8 all-to-all-done.3
  304.4 29.9 %all_to_all.46 = bf16[16,5,7168]{2,1,0:T(8,128)(2,1)S(1)} all-to-all(bf16[16,5,7168]{2,1,0:T(8,128)(2,1)S(1)} %reshape.207), channel_id=1, replica_groups=mesh['dp'=8,'tp'=16] {'tp'}, dimensions={0} | all-to-all | bytes 2293760 | tf_op jit(solution)/shard_map/all_to_all | solution.py:141
  334.3 1.8 copy.74
  336.2 49.3 %all-gather.2.cloned.1.call-done = bf16[128,5,7168]{2,0,1:T(8,128)(2,1)} async-done(((bf16[16,5,7168]{2,0,1:T(8,128)(2,1)}), bf16[128,5,7168]{2,0,1:T(8,128)(2,1)}) %all-gather.2.cloned.1.call-update) | async-done | bytes 9175056 | tf_op jit(solution)/shard_map/all_gather | solution.py:142
  385.5 14.0 %copy.75 = bf16[128,5,7168]{2,1,0:T(8,128)(2,1)} copy(bf16[128,5,7168]{2,0,1:T(8,128)(2,1)} %all-gather.2.cloned.1.call-done) | data formatting | bytes 18350080 | tf_op jit(solution)/shard_map/all_gather | solution.py:142
  399.5 15.1 %reshape.208 = bf16[640,7168]{1,0:T(8,128)(2,1)} reshape(bf16[128,5,7168]{2,1,0:T(8,128)(2,1)} %copy.75) | data formatting | bytes 18350080 | tf_op jit(solution)/shard_map/reshape | solution.py:143
  414.6 7.2 %fusion.8 = f32[640,256]{1,0:T(8,128)S(1)} fusion(bf16[640,7168]{1,0:T(8,128)(2,1)} %reshape.208, bf16[1,7168,256]{2,1,0:T(8,128)(2,1)} %param.31), kind=kOutput, calls=%fused_computation.16 | convolution fusion | flops 2348810240 | bytes 13500416 | tf_op jit(solution)/shard_map/dot_general | solution.py:145
  421.8 18.9 %convolution_convert_fusion = bf16[640,7168]{1,0:T(8,128)(2,1)} fusion(bf16[1,256,7168]{2,1,0:T(8,128)(2,1)} %param.33, bf16[640,7168]{1,0:T(8,128)(2,1)} %reshape.208, bf16[1,7168,256]{2,1,0:T(8,128)(2,1)} %param.32, f32[640,256]{1,0:T(8,128)S(1)} %fusion.8), kind=kOutput, calls=%fused_computation.1 | convolution fusion | flops 4703191040 | bytes 26345472 | tf_op jit(solution)/shard_map/dot_general | solution.py:149
  443.3 4.9 select_select_fusion
  448.2 7.2 %all-to-all-start = ((bf16[16,2,256,576]{2,3,1,0:T(8,128)(2,1)}), bf16[16,2,256,576]{2,3,1,0:T(8,128)(2,1)}, u32[]{:S(2)}, u32[]{:S(2)}) async-start(bf16[16,2,256,576]{2,3,1,0:T(8,128)(2,1)} %select_select_fusion), calls=%async_computation | async-start | bytes 18874368 | tf_op jit(solution)/shard_map/all_to_all | solution.py:75
  464.8 1.4 pad_add_fusion
  466.5 2.2 fusion.88
  469.5 1.6 add_convert_fusion
  471.1 148.7 %all-to-all-done = bf16[16,2,256,576]{2,3,1,0:T(8,128)(2,1)} async-done(((bf16[16,2,256,576]{2,3,1,0:T(8,128)(2,1)}), bf16[16,2,256,576]{2,3,1,0:T(8,128)(2,1)}, u32[]{:S(2)}, u32[]{:S(2)}) %all-to-all-start) | async-done | bytes 9437216 | tf_op jit(solution)/shard_map/all_to_all | solution.py:75
  622.3 2.6 reshape.209
  624.9 10.5 %all-to-all-start.5 = ((bf16[16,5,7168]{2,1,0:T(8,128)(2,1)}), bf16[16,5,7168]{2,1,0:T(8,128)(2,1)S(1)}, u32[]{:S(2)}, u32[]{:S(2)}) async-start(bf16[16,5,7168]{2,1,0:T(8,128)(2,1)} %reshape.209), calls=%async_computation.7 | async-start | bytes 3670016 | tf_op jit(solution)/shard_map/all_to_all | solution.py:155
  638.3 23.0 %all-to-all-done.5 = bf16[16,5,7168]{2,1,0:T(8,128)(2,1)S(1)} async-done(((bf16[16,5,7168]{2,1,0:T(8,128)(2,1)}), bf16[16,5,7168]{2,1,0:T(8,128)(2,1)S(1)}, u32[]{:S(2)}, u32[]{:S(2)}) %all-to-all-start.5) | async-done | bytes 1146912 | tf_op jit(solution)/shard_map/all_to_all | solution.py:155
  661.9 2.1 gather_fusion
  663.9 1.6 fusion.31
  (100 shorter events, 16.5 us)
Async XLA Ops:
  7.2 123.8 %copy-start = (bf16[896,1152]{1,0:T(8,128)(2,1)S(1)}, bf16[896,1152]{1,0:T(8,128)(2,1)}, u32[]{:S(2)}) copy-start(bf16[896,1152]{1,0:T(8,128)(2,1)} %param.28) | copy-start | bytes 6193156
  7.2 202.9 %all-reduce.3.cloned.1.call-start = ((), (), s32[]{:S(2)}) async-start(), calls=%async_computation.11 | async-start | bytes 9437184 | tf_op jit(solution)/shard_map/psum | solution.py:109
  131.0 4.1 copy-start.16
  139.3 153.6 %reduce-scatter.3.cloned.1.call-start = ((), (), s32[]{:S(2)}) async-start(), calls=%async_computation.8 | async-start | bytes 1949696 | tf_op jit(solution)/shard_map/reduce_scatter | solution.py:113
  210.1 7.4 %copy-start.10 = (s32[8,8]{1,0:T(8,128)S(1)}, s32[8,8]{1,0:T(8,128)}, u32[]{:S(2)}) copy-start(s32[8,8]{1,0:T(8,128)} %param.34) | copy-start | bytes 772
  217.4 85.7 %copy-start.4 = (bf16[8,7168]{1,0:T(8,128)(2,1)S(1)}, bf16[8,7168]{1,0:T(8,128)(2,1)}, u32[]{:S(2)}) copy-start(bf16[8,7168]{1,0:T(8,128)(2,1)} %param.25) | copy-start | bytes 344068
  217.4 85.9 %copy-start.11 = (f32[7168]{0:T(1024)S(1)}, f32[7168]{0:T(1024)}, u32[]{:S(2)}) copy-start(f32[7168]{0:T(1024)} %param.30) | copy-start | bytes 86020
  292.9 10.2 %all-to-all-start.3 = ((bf16[8,8,896]{2,1,0:T(8,128)(2,1)}), bf16[8,8,896]{2,1,0:T(8,128)(2,1)S(1)}, u32[]{:S(2)}, u32[]{:S(2)}) async-start(bf16[8,8,896]{2,1,0:T(8,128)(2,1)} %bitcast.99), calls=%async_computation.4 | async-start | bytes 229376 | tf_op jit(solution)/shard_map/all_to_all | solution.py:119
  297.2 88.4 %all-gather.2.cloned.1.call-start = ((), (), s32[]{:S(2)}) async-start(), calls=%async_computation.9 | async-start | bytes 10321920 | tf_op jit(solution)/shard_map/all_gather | solution.py:142
  336.1 286.2 %reduce-scatter.5.cloned.1.call-start = ((), (), s32[]{:S(2)}) async-start(), calls=%async_computation.10 | async-start | bytes 10321920 | tf_op jit(solution)/shard_map/reduce_scatter | solution.py:148
  440.6 0.7 copy-start.13
  440.6 2.6 copy-start.3
  448.2 15.9 %copy-start.12 = (f32[8,8]{1,0:T(8,128)S(1)}, f32[8,8]{1,0:T(8,128)}, u32[]{:S(2)}) copy-start(f32[8,8]{1,0:T(8,128)} %param.35) | copy-start | bytes 772
  448.2 16.0 %copy-start.14 = (s32[128,2]{0,1:T(2,128)S(1)}, s32[128,2]{0,1:T(2,128)}, u32[]{:S(2)}) copy-start(s32[128,2]{0,1:T(2,128)} %param.23) | copy-start | bytes 3076
  448.2 18.0 %copy-start.15 = (s32[6]{0:T(128)S(1)}, s32[6]{0:T(128)}, u32[]{:S(2)}) copy-start(s32[6]{0:T(128)} %param.22) | copy-start | bytes 76
  448.2 18.1 %copy-start.9 = (bf16[8,576]{1,0:T(8,128)(2,1)S(1)}, bf16[8,576]{1,0:T(8,128)(2,1)}, u32[]{:S(2)}) copy-start(bf16[8,576]{1,0:T(8,128)(2,1)} %param.19) | copy-start | bytes 27652
  448.2 18.1 %copy-start.2 = (bf16[8,128,576]{1,2,0:T(8,128)(2,1)S(1)}, bf16[8,128,576]{1,2,0:T(8,128)(2,1)}, u32[]{:S(2)}) copy-start(bf16[8,128,576]{1,2,0:T(8,128)(2,1)} %param.18) | copy-start | bytes 3538948
  448.2 171.5 %all-to-all-start = ((bf16[16,2,256,576]{2,3,1,0:T(8,128)(2,1)}), bf16[16,2,256,576]{2,3,1,0:T(8,128)(2,1)}, u32[]{:S(2)}, u32[]{:S(2)}) async-start(bf16[16,2,256,576]{2,3,1,0:T(8,128)(2,1)} %select_select_fusion), calls=%async_computation | async-start | bytes 18874368 | tf_op jit(solution)/shard_map/all_to_all | solution.py:75
  466.5 2.9 copy-start.17
  621.2 3.7 copy-start.6
  624.9 36.4 %all-to-all-start.5 = ((bf16[16,5,7168]{2,1,0:T(8,128)(2,1)}), bf16[16,5,7168]{2,1,0:T(8,128)(2,1)S(1)}, u32[]{:S(2)}, u32[]{:S(2)}) async-start(bf16[16,5,7168]{2,1,0:T(8,128)(2,1)} %reshape.209), calls=%async_computation.7 | async-start | bytes 3670016 | tf_op jit(solution)/shard_map/all_to_all | solution.py:155
  635.4 1.2 copy-start.8
  635.4 1.4 copy-start.7
  635.5 1.8 copy-start.5
  661.9 4.4 copy-start.1
Sparse Core Ops, SparseCore 0:
  139.4 70.6 all-reduce.2
  217.5 75.3 reduce-scatter.2
  336.2 49.2 all-gather.1
  440.8 56.3 reduce-scatter.4
